TPU v7x, 32 devices: a whole 2x2x4 slice. The times are simulated.
32 devices in a mesh: grp: 4 (over y, x), dev: 8 (over z, core).
Axes of the slice: x: 2, y: 2, z: 4, core: 2. Of those that a mesh axis runs over, the one named last changes fastest.
Arguments:
- reach: bfloat16 [128, 64, 1326], P(('grp', 'dev')), may hold values from 0.00029945374 to 0.0029907227
- stake: float32 [128], replicated, may hold values from 1 to 10
- hand_rank: int32 [64, 1326], P(('grp', 'dev')), may hold values from 0 to 7461
- hand_live: int32 [64, 1326], P(('grp', 'dev')), may hold values 0 or 1
- board_seqs: int32 [64], P(('grp', 'dev')), may hold values from 1 to 128, 4096 in all
- board_turn: int32 [64, 1], replicated, may hold values from 0 to 15
- seq_parent: int32 [128], replicated, may hold values from 0 to 31, never falling along the last dimension, each value on 1 to 8 neighbouring positions
- set_parent: int32 [32], replicated, may hold values from 0 to 7, never falling along the last dimension, each value on 1 to 8 neighbouring positions
Outputs:
- river_values: float32 [32, 64, 1326], P(None, ('grp', 'dev'))
- turn_values: float32 [8, 16, 1326], replicated
Inputs may be any that keep to these rules, and one draw needn't show every extreme that they name: `seq_parent`: Non-decreasing; every value occurs, at most 8 times, exactly 8 times for some value. `set_parent`: Non-decreasing; every value occurs, at most 8 times, exactly 8 times for some value. `board_seqs`: some board has all 128 sequences live. `board_turn`: every turn board has at least one river board.
All inputs are finite; a program needn't handle non-finite values. No bound on the sum of `hand_live` or of `board_seqs` on one device may be relied on, other than what follows from the above.
Results may differ from a plain program's by a relative error of at most 0.0003.
Values may be sent and summed in bfloat16 or wider, within the bound.
A program may use at most 64 MiB of HBM per device.

v0:
```python
import jax
import jax.numpy as jnp
import numpy as np
from jax import lax
from jax.sharding import PartitionSpec as P

TURNS = 16
KIDS = 8


def hand_cards(count):
    card_pairs = [
        (lower_card, upper_card)
        for lower_card in range(52)
        for upper_card in range(lower_card + 1, 52)
    ]
    table = np.array(card_pairs[:count], dtype=np.int32)
    return (jnp.asarray(table[:, 0]), jnp.asarray(table[:, 1]))


def apart_table(count):
    first_card, second_card = hand_cards(count)
    return (
        (first_card[:, None] != first_card[None, :])
        & (first_card[:, None] != second_card[None, :])
        & (second_card[:, None] != first_card[None, :])
        & (second_card[:, None] != second_card[None, :])
    )


def payoff_matrix(ranks, live, apart):
    both_live = live[:, None] * live[None, :] > 0
    signs = jnp.sign(ranks[:, None] - ranks[None, :]).astype(jnp.bfloat16)
    return jnp.where(apart & both_live, signs, jnp.bfloat16(0.0))


def children(parent, count_sets, most):
    set_iota = jnp.arange(count_sets, dtype=jnp.int32)
    counts = jnp.sum((parent[None, :] == set_iota[:, None]).astype(jnp.int32), axis=1)
    starts = jnp.cumsum(counts) - counts
    kid_iota = jnp.arange(most, dtype=jnp.int32)
    index = jnp.minimum(starts[:, None] + kid_iota[None, :], parent.shape[0] - 1)
    valid = kid_iota[None, :] < counts[:, None]
    return (index, valid)


def segment_best(values, index, valid):
    picked = values[index]
    shape = valid.shape + (1,) * (values.ndim - 1)
    return jnp.max(jnp.where(valid.reshape(shape), picked, -jnp.inf), axis=1)


def local(reach, stake, hand_rank, hand_live, board_seqs, board_turn, seq_parent, set_parent):
    moved = lax.all_to_all(reach, ("grp", "dev"), split_axis=1, concat_axis=0, tiled=True)
    total_seqs = moved.shape[0]
    local_boards = moved.shape[1]
    hands = moved.shape[2]
    river_sets = set_parent.shape[0]
    apart = apart_table(hands)
    kid_index, kid_valid = children(seq_parent, river_sets, KIDS)
    seq_iota = jnp.arange(total_seqs, dtype=jnp.int32)
    river_list = []
    for board in range(local_boards):
        live_rows = (seq_iota < board_seqs[board]).astype(jnp.bfloat16)
        rows = moved[:, board, :] * live_rows[:, None]
        matrix = payoff_matrix(hand_rank[board], hand_live[board], apart)
        product = lax.dot_general(
            rows, matrix, (((1,), (1,)), ((), ())), preferred_element_type=jnp.float32
        )
        leaf = product * stake[:, None]
        river_list.append(segment_best(leaf, kid_index, kid_valid))
    river = jnp.stack(river_list, axis=1)
    turn_iota = jnp.arange(TURNS, dtype=jnp.int32)
    devices = lax.axis_size(("grp", "dev"))
    owned_sets = river_sets // devices
    owned = lax.all_to_all(river, ("grp", "dev"), split_axis=0, concat_axis=1, tiled=True)
    onehot = (board_turn[:, 0][None, :] == turn_iota[:, None]).astype(jnp.float32)
    chance = jnp.einsum("tb,pbh->pth", onehot, owned, precision=lax.Precision.HIGHEST)
    set_count = river_sets // 4
    set_iota = jnp.arange(set_count, dtype=jnp.int32)
    first_set = lax.axis_index(("grp", "dev")) * owned_sets
    parent_set = set_parent[first_set + 0]
    chosen = (set_iota == parent_set)[:, None, None]
    candidate = jnp.where(chosen, chance[0][None], -jnp.inf)
    best = lax.pmax(candidate, ("grp", "dev"))
    return (river, best)


def solution(mesh):
    in_specs = (
        P(("grp", "dev"), None, None),
        P(),
        P(("grp", "dev"), None),
        P(("grp", "dev"), None),
        P(("grp", "dev")),
        P(),
        P(),
        P(),
    )
    out_specs = (P(None, ("grp", "dev"), None), P())
    return jax.shard_map(local, mesh=mesh, in_specs=in_specs, out_specs=out_specs, check_vma=False)
```

profile of v0, /device:TPU:0, one launch (start us, length us, event | category | flops | bytes accessed | tf_op | source)
XLA Modules:
  0.0 209.9 jit_solution(5315465424213060597)
XLA Ops:
  7.2 2.5 %copy.39 = bf16[4,64,1326]{2,0,1:T(4,128)(2,1)} copy(bf16[4,64,1326]{2,1,0:T(8,128)(2,1)} %param.10) | data formatting | bytes 1357824 | tf_op args[0]
  9.8 7.3 %all-to-all-start = ((bf16[4,64,1326]{2,0,1:T(4,128)(2,1)}), bf16[4,64,1326]{2,0,1:T(4,128)(2,1)S(1)}, u32[]{:S(2)}, u32[]{:S(2)}) async-start(bf16[4,64,1326]{2,0,1:T(4,128)(2,1)} %copy.39), calls=%async_computation | async-start | bytes 1441792 | tf_op jit(solution)/shard_map/all_to_all | solution.py:54
  17.1 0.1 convert_reduce_fusion
  17.2 0.1 copy.42
  17.3 0.1 reduce.2
  17.5 0.1 compare_select_fusion
  17.5 0.1 reshape.133
  17.6 0.6 fusion.26
  18.2 0.6 compare_convert_fusion
  18.9 0.7 compare_convert_fusion.1
  19.8 17.9 %all-to-all-done = bf16[4,64,1326]{2,0,1:T(4,128)(2,1)S(1)} async-done(((bf16[4,64,1326]{2,0,1:T(4,128)(2,1)}), bf16[4,64,1326]{2,0,1:T(4,128)(2,1)S(1)}, u32[]{:S(2)}, u32[]{:S(2)}) %all-to-all-start) | async-done | bytes 678944 | tf_op jit(solution)/shard_map/all_to_all | solution.py:54
  37.6 0.6 copy.40
  38.2 1.0 fusion.25
  39.2 1.0 copy.44
  40.2 4.6 %fusion.11 = f32[128,1326]{0,1:T(8,128)S(1)} fusion(s32[1326]{0:T(1024)S(1)} %get-tuple-element.13, s32[1326]{0:T(1024)S(1)} %get-tuple-element.20, s32[1326]{0:T(1024)S(1)} %copy-done.8, s32[1326]{0:T(1024)S(1)} %copy-done.7, bf16[128,1,1326]{0,2,1:T(8,128)(2,1)S(1)} %copy.44, f32[128]{0:T(128)S(1)} %copy-done.5, bf16[128]{0:T(256)(128)(2,1)S(1)} %compare_convert_fusion), kind=kOutput, calls=%fused_computation.14 | convolution fusion | flops 475073984 | bytes 1040352 | tf_op jit(solution)/shard_map/dot_general | solution.py:67
  44.9 0.3 copy.45
  45.1 1.2 copy.41
  46.3 4.6 %fusion.8 = f32[128,1326]{0,1:T(8,128)S(1)} fusion(s32[1326]{0:T(1024)S(1)} %get-tuple-element.12, s32[1326]{0:T(1024)S(1)} %get-tuple-element.21, s32[1326]{0:T(1024)S(1)} %copy-done.8, s32[1326]{0:T(1024)S(1)} %copy-done.7, bf16[128,1,1326]{0,2,1:T(8,128)(2,1)S(1)} %copy.41, f32[128]{0:T(128)S(1)} %copy-done.5, bf16[128]{0:T(256)(128)(2,1)S(1)} %compare_convert_fusion.1), kind=kOutput, calls=%fused_computation.13 | convolution fusion | flops 475073984 | bytes 1040352 | tf_op jit(solution)/shard_map/dot_general | solution.py:67
  50.9 0.3 copy.43
  51.2 1.2 gather_fusion.1
  52.5 2.3 %gather_fusion = f32[256,1326]{1,0:T(8,128)} fusion(f32[128,1326]{1,0:T(8,128)S(1)} %copy.43, s32[1024]{0:T(1024)S(1)} %pad_clamp_fusion), kind=kCustom, calls=%fused_computation | custom fusion | bytes 2716672 | tf_op jit(solution)/shard_map/gather | solution.py:48
  54.8 2.3 %fusion.17 = (f32[32,1326]{1,0:T(8,128)S(1)}, f32[32,1326]{1,0:T(8,128)S(1)}) fusion(f32[256,1326]{1,0:T(8,128)} %gather_fusion, pred[32,8]{1,0:T(8,128)(4,1)S(1)} %iota_compare_fusion.1, f32[256,1326]{1,0:T(8,128)S(1)} %gather_fusion.1), kind=kLoop, calls=%fused_computation.21 | loop fusion | flops 1272960 | bytes 3055360 | tf_op jit(solution)/shard_map/reduce_max | solution.py:50
  57.1 1.0 copy.47
  58.2 2.6 %all-to-all-start.1 = ((f32[32,2,1326]{2,1,0:T(2,128)}), f32[32,2,1326]{2,1,0:T(2,128)S(1)}, u32[]{:S(2)}, u32[]{:S(2)}) async-start(f32[32,2,1326]{2,1,0:T(2,128)} %copy.47), calls=%async_computation.1 | async-start | bytes 720896 | tf_op jit(solution)/shard_map/all_to_all | solution.py:76
  60.8 0.6 dynamic_slice.3
  61.4 0.6 iota_compare_fusion.4
  62.1 11.5 %all-to-all-done.1 = f32[32,2,1326]{2,1,0:T(2,128)S(1)} async-done(((f32[32,2,1326]{2,1,0:T(2,128)}), f32[32,2,1326]{2,1,0:T(2,128)S(1)}, u32[]{:S(2)}, u32[]{:S(2)}) %all-to-all-start.1) | async-done | bytes 339488 | tf_op jit(solution)/shard_map/all_to_all | solution.py:76
  73.6 0.2 reshape.130
  73.9 0.2 convolution_bitcast_fusion
  74.1 1.0 broadcast_select_fusion
  75.1 125.9 %all-reduce.2.cloned.1.call-done = f32[8,16,1326]{2,1,0:T(8,128)} async-done(((f32[8,16,1326]{2,1,0:T(8,128)}), f32[8,16,1326]{2,1,0:T(8,128)}) %all-reduce.2.cloned.1.call-update) | async-done | bytes 678928 | tf_op jit(solution)/shard_map/pmax | solution.py:85
  201.0 2.0 copy.49
  (26 shorter events, 0.3 us)
Async XLA Ops:
  7.2 9.9 %copy-start.4 = (s32[128]{0:T(128)S(1)}, s32[128]{0:T(128)}, u32[]{:S(2)}) copy-start(s32[128]{0:T(128)} %param.16) | copy-start | bytes 1540
  7.2 10.5 %copy-start.2 = (s32[2]{0:T(128)S(1)}, s32[2]{0:T(128)}, u32[]{:S(2)}) copy-start(s32[2]{0:T(128)} %param.14) | copy-start | bytes 28
  7.2 12.4 %copy-start = (s32[2,1326]{1,0:T(2,128)S(1)}, s32[2,1326]{1,0:T(2,128)}, u32[]{:S(2)}) copy-start(s32[2,1326]{1,0:T(2,128)} %param.12) | copy-start | bytes 31828
  7.2 12.4 %copy-start.1 = (s32[2,1326]{1,0:T(2,128)S(1)}, s32[2,1326]{1,0:T(2,128)}, u32[]{:S(2)}) copy-start(s32[2,1326]{1,0:T(2,128)} %param.13) | copy-start | bytes 31828
  9.8 27.9 %all-to-all-start = ((bf16[4,64,1326]{2,0,1:T(4,128)(2,1)}), bf16[4,64,1326]{2,0,1:T(4,128)(2,1)S(1)}, u32[]{:S(2)}, u32[]{:S(2)}) async-start(bf16[4,64,1326]{2,0,1:T(4,128)(2,1)} %copy.39), calls=%async_computation | async-start | bytes 1441792 | tf_op jit(solution)/shard_map/all_to_all | solution.py:54
  38.2 2.0 copy-start.5
  38.2 2.0 copy-start.7
  38.2 2.0 copy-start.8
  57.1 3.7 %copy-start.6 = (s32[32]{0:T(128)S(1)}, s32[32]{0:T(128)}, u32[]{:S(2)}) copy-start(s32[32]{0:T(128)} %param.17) | copy-start | bytes 388
  57.1 16.8 %copy-start.3 = (s32[64,1]{0,1:T(1,128)S(1)}, s32[64,1]{0,1:T(1,128)}, u32[]{:S(2)}) copy-start(s32[64,1]{0,1:T(1,128)} %param.15) | copy-start | bytes 772
  58.2 15.4 %all-to-all-start.1 = ((f32[32,2,1326]{2,1,0:T(2,128)}), f32[32,2,1326]{2,1,0:T(2,128)S(1)}, u32[]{:S(2)}, u32[]{:S(2)}) async-start(f32[32,2,1326]{2,1,0:T(2,128)} %copy.47), calls=%async_computation.1 | async-start | bytes 720896 | tf_op jit(solution)/shard_map/all_to_all | solution.py:76
  60.8 140.3 %all-reduce.2.cloned.1.call-start = ((), (), s32[]{:S(2)}) async-start(), calls=%async_computation.2 | async-start | bytes 1441792 | tf_op jit(solution)/shard_map/pmax | solution.py:85
Sparse Core Ops, SparseCore 0:
  75.2 125.7 all-reduce.1
where the time goes:
time: 210 us
  waiting for transfers between devices  155 us (74%)
  local copies, waits for them, and re-layouts  15.1 us (7%)
  between operations  14.3 us (7%)
  starting transfers between devices  9.93 us (5%)
  matrix products  9.5 us (5%)
  other arithmetic  5.76 us (3%)
    pmax x1, waiting for transfers between devices, local(): best = lax.pmax(candidate, ('grp', 'dev'))  126 us
    all_to_all x1, waiting for transfers between devices, local(): lax.all_to_all(reach, ('grp', 'dev'), split_axis=1, concat_axis=0, tiled=...  17.9 us
    all_to_all x1, waiting for transfers between devices, local(): lax.all_to_all(river, ('grp', 'dev'), split_axis=0, concat_axis=1, tiled=...  11.5 us
    dot_general x2, matrix products, local(): lax.dot_general(rows, matrix, (((1,), (1,)), ((), ())), preferred_element...  9.25 us
    all_to_all x1, starting transfers between devices, local(): lax.all_to_all(reach, ('grp', 'dev'), split_axis=1, concat_axis=0, tiled=...  7.3 us
    unnamed x21, local copies, waits for them, and re-layouts  5.63 us
  transfers between devices with their start and end apart: 3, of which 3 were waited for; matrix products, arithmetic and copies ran while one was open for 2% of the time, Pallas kernels for 0%

commit v1 on v0

--- a/solution.py
+++ b/solution.py
@@ -51,7 +51,12 @@
 
 
 def local(reach, stake, hand_rank, hand_live, board_seqs, board_turn, seq_parent, set_parent):
-    moved = lax.all_to_all(reach, ("grp", "dev"), split_axis=1, concat_axis=0, tiled=True)
+    moved = jnp.concatenate(
+        lax.all_to_all(
+            jnp.stack(jnp.split(reach, lax.axis_size(("grp", "dev")), axis=1)), ("grp", "dev"), 0, 0
+        ),
+        axis=0,
+    )
     total_seqs = moved.shape[0]
     local_boards = moved.shape[1]
     hands = moved.shape[2]

time: 210 us -> 257 us (1.22)
  local copies, waits for them, and re-layouts: 15.1 us -> 60.6 us
    unnamed x21 -> x51, local copies, waits for them, and re-layouts: 5.63 us -> 50.2 us
where the time goes in v1:
time: 257 us; the launch traced here: 255 us
  waiting for transfers between devices  155 us (60%)
  local copies, waits for them, and re-layouts  60.6 us (24%)
  between operations  14.3 us (6%)
  starting transfers between devices  9.93 us (4%)
  matrix products  9.48 us (4%)
  other arithmetic  5.76 us (2%)
    pmax x1, waiting for transfers between devices, local(): best = lax.pmax(candidate, ('grp', 'dev'))  126 us
    unnamed x51, local copies, waits for them, and re-layouts  50.2 us
    all_to_all x1, waiting for transfers between devices, local(): lax.all_to_all(jnp.stack(jnp.split(reach, lax.axis_size(('grp', 'dev')),...  17.9 us
    all_to_all x1, waiting for transfers between devices, local(): lax.all_to_all(river, ('grp', 'dev'), split_axis=0, concat_axis=1, tiled=...  11.5 us
    dot_general x2, matrix products, local(): lax.dot_general(rows, matrix, (((1,), (1,)), ((), ())), preferred_element...  9.24 us
    all_to_all x1, starting transfers between devices, local(): lax.all_to_all(jnp.stack(jnp.split(reach, lax.axis_size(('grp', 'dev')),...  7.3 us
  transfers between devices with their start and end apart: 3, of which 3 were waited for; matrix products, arithmetic and copies ran while one was open for 2% of the time, Pallas kernels for 0%

profile of v1, /device:TPU:0, one launch (start us, length us, event | category | flops | bytes accessed | tf_op | source)
XLA Modules:
  0.0 255.4 jit_solution(10715277764195847284)
XLA Ops:
  8.7 1.5 constant_dynamic-update-slice_fusion.30
  10.2 1.5 constant_dynamic-update-slice_fusion.29
  11.8 1.5 constant_dynamic-update-slice_fusion.28
  14.8 1.5 constant_dynamic-update-slice_fusion.26
  16.3 1.5 constant_dynamic-update-slice_fusion.25
  17.9 1.5 constant_dynamic-update-slice_fusion.24
  20.9 1.5 constant_dynamic-update-slice_fusion.22
  22.4 1.5 constant_dynamic-update-slice_fusion.21
  27.0 1.5 constant_dynamic-update-slice_fusion.18
  28.5 1.5 constant_dynamic-update-slice_fusion.17
  30.0 1.5 constant_dynamic-update-slice_fusion.16
  33.0 1.5 constant_dynamic-update-slice_fusion.14
  34.6 1.5 constant_dynamic-update-slice_fusion.13
  36.1 1.5 constant_dynamic-update-slice_fusion.12
  39.1 1.5 constant_dynamic-update-slice_fusion.10
  40.6 1.5 constant_dynamic-update-slice_fusion.9
  42.2 1.5 constant_dynamic-update-slice_fusion.8
  45.2 1.5 constant_dynamic-update-slice_fusion.6
  46.7 1.5 constant_dynamic-update-slice_fusion.5
  48.2 1.5 constant_dynamic-update-slice_fusion.4
  52.8 1.5 constant_dynamic-update-slice_fusion.1
  54.3 1.5 constant_dynamic-update-slice_fusion
  55.8 7.3 %all-to-all-start = ((bf16[32,4,2,1326]{3,2,1,0:T(2,128)(2,1)}), bf16[32,4,2,1326]{3,2,1,0:T(2,128)(2,1)S(1)}, u32[]{:S(2)}, u32[]{:S(2)}) async-start(bf16[32,4,2,1326]{3,2,1,0:T(2,128)(2,1)} %constant_dynamic-update-slice_fusion), calls=%async_computation | async-start | bytes 1441792 | tf_op jit(solution)/shard_map/all_to_all | solution.py:55
  65.9 17.9 %all-to-all-done = bf16[32,4,2,1326]{3,2,1,0:T(2,128)(2,1)S(1)} async-done(((bf16[32,4,2,1326]{3,2,1,0:T(2,128)(2,1)}), bf16[32,4,2,1326]{3,2,1,0:T(2,128)(2,1)S(1)}, u32[]{:S(2)}, u32[]{:S(2)}) %all-to-all-start) | async-done | bytes 678944 | tf_op jit(solution)/shard_map/all_to_all | solution.py:55
  85.7 4.6 %fusion.11 = f32[128,1326]{0,1:T(8,128)S(1)} fusion(s32[1326]{0:T(1024)S(1)} %get-tuple-element.13, s32[1326]{0:T(1024)S(1)} %get-tuple-element.20, s32[1326]{0:T(1024)S(1)} %copy-done.8, s32[1326]{0:T(1024)S(1)} %copy-done.7, bf16[128,1,1326]{0,2,1:T(8,128)(2,1)S(1)} %copy.37, f32[128]{0:T(128)S(1)} %copy-done.5, bf16[128]{0:T(256)(128)(2,1)S(1)} %compare_convert_fusion), kind=kOutput, calls=%fused_computation.14 | convolution fusion | flops 475073984 | bytes 1040352 | tf_op jit(solution)/shard_map/dot_general | solution.py:72
  91.8 4.6 %fusion.8 = f32[128,1326]{0,1:T(8,128)S(1)} fusion(s32[1326]{0:T(1024)S(1)} %get-tuple-element.12, s32[1326]{0:T(1024)S(1)} %get-tuple-element.21, s32[1326]{0:T(1024)S(1)} %copy-done.8, s32[1326]{0:T(1024)S(1)} %copy-done.7, bf16[128,1,1326]{0,2,1:T(8,128)(2,1)S(1)} %copy.34, f32[128]{0:T(128)S(1)} %copy-done.5, bf16[128]{0:T(256)(128)(2,1)S(1)} %compare_convert_fusion.1), kind=kOutput, calls=%fused_computation.13 | convolution fusion | flops 475073984 | bytes 1040352 | tf_op jit(solution)/shard_map/dot_general | solution.py:72
  97.9 2.3 gather_fusion
  100.2 2.3 fusion.17
  103.6 2.6 %all-to-all-start.1 = ((f32[32,2,1326]{2,1,0:T(2,128)}), f32[32,2,1326]{2,1,0:T(2,128)S(1)}, u32[]{:S(2)}, u32[]{:S(2)}) async-start(f32[32,2,1326]{2,1,0:T(2,128)} %copy.40), calls=%async_computation.1 | async-start | bytes 720896 | tf_op jit(solution)/shard_map/all_to_all | solution.py:81
  107.5 11.5 %all-to-all-done.1 = f32[32,2,1326]{2,1,0:T(2,128)S(1)} async-done(((f32[32,2,1326]{2,1,0:T(2,128)}), f32[32,2,1326]{2,1,0:T(2,128)S(1)}, u32[]{:S(2)}, u32[]{:S(2)}) %all-to-all-start.1) | async-done | bytes 339488 | tf_op jit(solution)/shard_map/all_to_all | solution.py:81
  120.6 125.9 %all-reduce.2.cloned.1.call-done = f32[8,16,1326]{2,1,0:T(8,128)} async-done(((f32[8,16,1326]{2,1,0:T(8,128)}), f32[8,16,1326]{2,1,0:T(8,128)}) %all-reduce.2.cloned.1.call-update) | async-done | bytes 678928 | tf_op jit(solution)/shard_map/pmax | solution.py:90
  246.5 2.0 copy.73
  (56 shorter events, 26.5 us)
Async XLA Ops:
  7.2 56.0 %copy-start.4 = (s32[128]{0:T(128)S(1)}, s32[128]{0:T(128)}, u32[]{:S(2)}) copy-start(s32[128]{0:T(128)} %param.16) | copy-start | bytes 1540
  10.2 53.5 %copy-start.2 = (s32[2]{0:T(128)S(1)}, s32[2]{0:T(128)}, u32[]{:S(2)}) copy-start(s32[2]{0:T(128)} %param.14) | copy-start | bytes 28
  11.7 53.9 %copy-start = (s32[2,1326]{1,0:T(2,128)S(1)}, s32[2,1326]{1,0:T(2,128)}, u32[]{:S(2)}) copy-start(s32[2,1326]{1,0:T(2,128)} %param.12) | copy-start | bytes 31828
  11.8 54.0 %copy-start.1 = (s32[2,1326]{1,0:T(2,128)S(1)}, s32[2,1326]{1,0:T(2,128)}, u32[]{:S(2)}) copy-start(s32[2,1326]{1,0:T(2,128)} %param.13) | copy-start | bytes 31828
  55.8 27.9 %all-to-all-start = ((bf16[32,4,2,1326]{3,2,1,0:T(2,128)(2,1)}), bf16[32,4,2,1326]{3,2,1,0:T(2,128)(2,1)S(1)}, u32[]{:S(2)}, u32[]{:S(2)}) async-start(bf16[32,4,2,1326]{3,2,1,0:T(2,128)(2,1)} %constant_dynamic-update-slice_fusion), calls=%async_computation | async-start | bytes 1441792 | tf_op jit(solution)/shard_map/all_to_all | solution.py:55
  83.7 2.0 copy-start.5
  83.7 2.0 copy-start.7
  83.7 2.0 copy-start.8
  102.6 3.7 %copy-start.6 = (s32[32]{0:T(128)S(1)}, s32[32]{0:T(128)}, u32[]{:S(2)}) copy-start(s32[32]{0:T(128)} %param.17) | copy-start | bytes 388
  102.6 16.8 %copy-start.3 = (s32[64,1]{0,1:T(1,128)S(1)}, s32[64,1]{0,1:T(1,128)}, u32[]{:S(2)}) copy-start(s32[64,1]{0,1:T(1,128)} %param.15) | copy-start | bytes 772
  103.6 15.4 %all-to-all-start.1 = ((f32[32,2,1326]{2,1,0:T(2,128)}), f32[32,2,1326]{2,1,0:T(2,128)S(1)}, u32[]{:S(2)}, u32[]{:S(2)}) async-start(f32[32,2,1326]{2,1,0:T(2,128)} %copy.40), calls=%async_computation.1 | async-start | bytes 720896 | tf_op jit(solution)/shard_map/all_to_all | solution.py:81
  106.2 140.3 %all-reduce.2.cloned.1.call-start = ((), (), s32[]{:S(2)}) async-start(), calls=%async_computation.2 | async-start | bytes 1441792 | tf_op jit(solution)/shard_map/pmax | solution.py:90
Sparse Core Ops, SparseCore 0:
  120.7 125.7 all-reduce.1
